TPU v7x, 32 devices: a whole 2x2x4 slice. The times are simulated.
32 devices in a mesh: dp: 4 (over y, x), ctx: 2 (over core), tp: 4 (over z).
Axes of the slice: x: 2, y: 2, z: 4, core: 2. Of those that a mesh axis runs over, the one named last changes fastest.
Arguments:
- block_input_activations: bfloat16 [8192, 1024], P(('dp', 'ctx')), may hold values from -6 to 6
- sequence_first_token: int32 [8192], P(('dp', 'ctx')), may hold values from 0 to 1, as said below
- norm_gain: float32 [1024], replicated, may hold values from 0.5 to 1.5
- gate_proj: bfloat16 [1024, 2048], P(('dp', 'ctx'), 'tp'), may hold values from -0.1875 to 0.1875
- input_proj: bfloat16 [1024, 2048], P(('dp', 'ctx'), 'tp'), may hold values from -0.1875 to 0.1875
- step_proj: bfloat16 [1024, 32], P(('dp', 'ctx'), 'tp'), may hold values from -0.1875 to 0.1875
- state_proj: bfloat16 [1024, 256], P(('dp', 'ctx')), may hold values from -0.1875 to 0.1875
- conv_inner_weight: float32 [4, 2048], P(None, 'tp'), may hold values from -3 to 3
- conv_inner_bias: float32 [2048], P('tp'), may hold values from -0.5 to 0.5
- conv_state_weight: float32 [4, 256], replicated, may hold values from -3 to 3
- conv_state_bias: float32 [256], replicated, may hold values from -0.5 to 0.5
- step_bias: float32 [32], P('tp'), may hold values from -6 to -2
- decay_log: float32 [32], P('tp'), may hold values from 0 to 2.5
- skip_weight: float32 [32], P('tp'), may hold values from 0.5 to 1.5
- gate_gain: float32 [2048], P('tp'), may hold values from 0.5 to 1.5
- out_proj: bfloat16 [2048, 1024], P('tp', ('dp', 'ctx')), may hold values from -0.125 to 0.125
- output_cotangent: bfloat16 [8192, 1024], P(('dp', 'ctx')), may hold values from -6 to 6
Outputs:
- block_output: bfloat16 [8192, 1024], P(('dp', 'ctx'), 'tp')
- input_grad: float32 [8192, 1024], P(('dp', 'ctx'), 'tp')
- norm_gain_grad: float32 [1024], P('tp')
- gate_proj_grad: float32 [1024, 2048], P(('dp', 'ctx'), 'tp')
- input_proj_grad: float32 [1024, 2048], P(('dp', 'ctx'), 'tp')
- step_proj_grad: float32 [1024, 32], P(('dp', 'ctx'), 'tp')
- state_proj_grad: float32 [1024, 256], P(('dp', 'ctx'))
- conv_inner_weight_grad: float32 [4, 2048], P(None, 'tp')
- conv_inner_bias_grad: float32 [2048], P('tp')
- conv_state_weight_grad: float32 [4, 256], replicated
- conv_state_bias_grad: float32 [256], replicated
- step_bias_grad: float32 [32], P('tp')
- decay_log_grad: float32 [32], P('tp')
- skip_weight_grad: float32 [32], P('tp')
- gate_gain_grad: float32 [2048], P('tp')
- out_proj_grad: float32 [2048, 1024], P('tp', ('dp', 'ctx'))
Inputs may be any that keep to these rules, and one draw needn't show every extreme that they name: `sequence_first_token`: every packed row of 2048 tokens begins with a 1; every sequence has 1 to 1536 positions, and each row holds one of exactly 1536.
All inputs are finite; a program needn't handle non-finite values.
Results may differ from a plain program's by a relative error of at most 0.012.
Values may be sent and summed in bfloat16 or wider, within the bound.
A program may use at most 128 MiB of HBM per device.

v0:
```python
import jax
import jax.numpy as jnp
from jax import lax
from jax.sharding import PartitionSpec as P

MODEL_WIDTH = 1024
HEADDIM = 64
STATE = 128
KCONV = 4
SPAN = 256
INNER = 2048


EPSILON = 1e-05
HIGHEST = lax.Precision.HIGHEST


def passed_along(block, axis, distance):
    devices = range(lax.axis_size(axis))
    route = [(i - distance, i) for i in devices if i - distance in devices]
    return lax.ppermute(block, axis, route)


def prefix(part, axis, combine, identity, reverse):
    count = lax.axis_size(axis)
    place = lax.axis_index(axis)
    ahead = count - 1 - place if reverse else place
    gathered = jax.tree.map(lambda a: lax.all_gather(a, axis), part)
    state = jax.tree.map(lambda a, e: jnp.zeros_like(a) + jnp.asarray(e, a.dtype), part, identity)

    def one(lap, state):
        source = count - 1 - lap if reverse else lap
        return combine(
            state, jax.tree.map(lambda a: lax.dynamic_index_in_dim(a, source, 0, False), gathered)
        )

    return lax.fori_loop(0, ahead, one, state)


def conv_apply(padded, flags_padded, conv_weight, conv_bias):
    width = KCONV - 1
    count = padded.shape[0] - width
    segments = jnp.cumsum(flags_padded)
    own = segments[width:]
    result = jnp.zeros((count, padded.shape[1]), jnp.float32) + conv_bias[None, :]
    for lag in range(KCONV):
        valid = (segments[width - lag : width - lag + count] == own).astype(jnp.float32)
        result = (
            result
            + conv_weight[lag][None, :] * padded[width - lag : width - lag + count] * valid[:, None]
        )
    return result


def span_parts(inner_values, step_size, state_in, state_out, sequence_starts, decay_rate):
    count = inner_values.shape[0]
    heads = step_size.shape[1]
    spans = count // SPAN
    log_decay = (step_size * decay_rate[None, :]).reshape(spans, SPAN, heads)
    cumulative = jnp.cumsum(log_decay, axis=1)
    segments = jnp.cumsum(sequence_starts.reshape(spans, SPAN), axis=1)
    block_values = inner_values.reshape(spans, SPAN, heads, HEADDIM)
    block_step = step_size.reshape(spans, SPAN, heads)
    block_in = state_in.reshape(spans, SPAN, STATE)
    block_out = state_out.reshape(spans, SPAN, STATE)
    order = jnp.arange(SPAN)
    lower = order[:, None] >= order[None, :]
    same = ((segments[:, :, None] == segments[:, None, :]) & lower[None])[..., None]
    spread = cumulative[:, :, None, :] - cumulative[:, None, :, :]
    decay = jnp.where(same, jnp.exp(jnp.where(same, spread, 0.0)), 0.0)
    scores = jnp.einsum("ktn,ksn->kts", block_out, block_in, precision=HIGHEST)
    mixing = decay * scores[..., None] * block_step[:, None, :, :]
    inner_mixed = jnp.einsum("ktsh,kshp->kthp", mixing, block_values, precision=HIGHEST)
    ending = (segments == segments[:, -1:])[..., None]
    to_end = jnp.where(ending, jnp.exp(cumulative[:, -1:, :] - cumulative), 0.0) * block_step
    states = jnp.einsum(
        "kshp,ksn->khpn", block_values * to_end[..., None], block_in, precision=HIGHEST
    )
    passing = jnp.where((segments == 0)[..., None], jnp.exp(cumulative), 0.0)
    return (inner_mixed, states, passing)


def fold_spans(states, passing):
    ends = passing[:, -1, :]

    def advance(carry, item):
        zero_state, product = carry
        state, end = item
        return ((end[:, None, None] * zero_state + state, end * product), (zero_state, product))

    init = (jnp.zeros(states.shape[1:], jnp.float32), jnp.ones(ends.shape[1:], jnp.float32))
    (final_state, final_product), (span_states, span_decays) = lax.scan(
        advance, init, (states, ends)
    )
    return (span_states, span_decays, final_state, final_product)


def mixer_front(
    padded, flags_padded, sequence_starts, step_raw, conv_weight, conv_bias, step_bias, decay_log
):
    inner_width = padded.shape[1] - 2 * STATE
    activated = jax.nn.silu(conv_apply(padded, flags_padded, conv_weight, conv_bias))
    inner_values = activated[:, :inner_width]
    state_in = activated[:, inner_width : inner_width + STATE]
    state_out = activated[:, inner_width + STATE :]
    step_size = jax.nn.softplus(step_raw + step_bias[None, :])
    decay_rate = -jnp.exp(decay_log)
    inner_mixed, states, passing = span_parts(
        inner_values, step_size, state_in, state_out, sequence_starts, decay_rate
    )
    span_states, span_decays, final_state, final_product = fold_spans(states, passing)
    kept = (inner_values, state_out, inner_mixed, passing, span_states, span_decays)
    return (kept, final_state, final_product)


def finish(kept, carried, skip):
    inner_values, state_out, inner_mixed, passing, span_states, span_decays = kept
    spans = inner_mixed.shape[0]
    heads = inner_mixed.shape[2]
    initial = span_states + span_decays[:, :, None, None] * carried[None]
    block_out = state_out.reshape(spans, SPAN, STATE)
    from_state = jnp.einsum("ktn,khpn->kthp", block_out, initial, precision=HIGHEST)
    block_values = inner_values.reshape(spans, SPAN, heads, HEADDIM)
    total = inner_mixed + passing[..., None] * from_state + skip[None, None, :, None] * block_values
    return total.reshape(inner_values.shape[0], heads * HEADDIM)


def mixer(
    padded,
    flags_padded,
    sequence_starts,
    step_raw,
    conv_weight,
    conv_bias,
    step_bias,
    decay_log,
    skip,
    carried,
):
    kept, final_state, final_product = mixer_front(
        padded,
        flags_padded,
        sequence_starts,
        step_raw,
        conv_weight,
        conv_bias,
        step_bias,
        decay_log,
    )
    output = finish(kept, carried, skip)
    return (output, final_state + final_product[:, None, None] * carried)


def chain_forward(earlier, later):
    return (earlier[0] * later[0], later[0][:, None, None] * earlier[1] + later[1])


def chain_backward(earlier, later):
    return (later[0] * earlier[0], later[1] + later[0][:, None, None] * earlier[1])


def on_device(
    block_input_activations,
    sequence_first_token,
    norm_gain,
    gate_proj,
    input_proj,
    step_proj,
    state_proj,
    conv_inner_weight,
    conv_inner_bias,
    conv_state_weight,
    conv_state_bias,
    step_bias,
    decay_log,
    skip_weight,
    gate_gain,
    out_proj,
    output_cotangent,
):
    full_gate, full_input, full_step, full_state, full_out = (
        lax.all_gather(gate_proj, ("dp", "ctx"), axis=0, tiled=True),
        lax.all_gather(input_proj, ("dp", "ctx"), axis=0, tiled=True),
        lax.all_gather(step_proj, ("dp", "ctx"), axis=0, tiled=True),
        lax.all_gather(state_proj, ("dp", "ctx"), axis=0, tiled=True),
        lax.all_gather(out_proj, ("dp", "ctx"), axis=1, tiled=True),
    )
    local_inner = full_gate.shape[1]
    width = KCONV - 1
    hidden = block_input_activations.astype(jnp.float32)
    inv_rms = lax.rsqrt(jnp.mean(hidden * hidden, axis=1, keepdims=True) + EPSILON)
    normed = (hidden * inv_rms * norm_gain[None, :]).astype(jnp.bfloat16)
    main_weight = jnp.concatenate([full_gate, full_input, full_state], axis=1)
    projected = jnp.dot(normed, main_weight, preferred_element_type=jnp.float32)
    step_raw = jnp.dot(normed, full_step, preferred_element_type=jnp.float32)
    gate = projected[:, :local_inner]
    conv_rows = projected[:, local_inner:].astype(jnp.bfloat16)
    sequence_starts = sequence_first_token.astype(jnp.float32)
    tail_rows, tail_flags = passed_along(
        (conv_rows[-width:], sequence_starts[-width:].astype(jnp.bfloat16)), "ctx", 1
    )
    padded = jnp.concatenate([tail_rows, conv_rows], axis=0).astype(jnp.float32)
    flags_padded = jnp.concatenate([tail_flags.astype(jnp.float32), sequence_starts])
    conv_weight = jnp.concatenate([conv_inner_weight, conv_state_weight], axis=1)
    conv_bias = jnp.concatenate([conv_inner_bias, conv_state_bias])
    kept, final_state, final_product = mixer_front(
        padded,
        flags_padded,
        sequence_starts,
        step_raw,
        conv_weight,
        conv_bias,
        step_bias,
        decay_log,
    )
    heads = step_bias.shape[0]
    identity = (jnp.ones((heads,), jnp.float32), jnp.zeros((heads, HEADDIM, STATE), jnp.float32))
    carried_decay, carried = prefix(
        (final_product, final_state), "ctx", chain_forward, identity, False
    )
    mixed = finish(kept, carried, skip_weight)
    gate_silu = jax.nn.silu(gate)
    gated = mixed * gate_silu
    square_sum = lax.psum(jnp.sum(gated * gated, axis=1), "tp")
    gate_inv = lax.rsqrt(square_sum / INNER + EPSILON)[:, None]
    gated_normed = (gated * gate_inv * gate_gain[None, :]).astype(jnp.bfloat16)
    share = MODEL_WIDTH // lax.axis_size("tp")
    column = lax.axis_index("tp") * share
    branch = lax.psum_scatter(
        jnp.dot(gated_normed, full_out, preferred_element_type=jnp.float32),
        "tp",
        scatter_dimension=1,
        tiled=True,
    )
    own_hidden = lax.dynamic_slice_in_dim(hidden, column, share, 1)
    block_output = (own_hidden + branch).astype(jnp.bfloat16)
    grad_gated_normed = jnp.dot(output_cotangent, full_out.T, preferred_element_type=jnp.float32)
    grad_out = jnp.dot(gated_normed.T, output_cotangent, preferred_element_type=jnp.float32)
    scaled = grad_gated_normed * gate_gain[None, :]
    dot_sum = lax.psum(jnp.sum(gated * scaled, axis=1), "tp")
    grad_gated = gate_inv * scaled - gated * gate_inv**3 * (dot_sum / INNER)[:, None]
    grad_gain_gate = jnp.sum(grad_gated_normed * gated * gate_inv, axis=0)
    sigmoid_gate = jax.nn.sigmoid(gate)
    grad_mixed = grad_gated * gate_silu
    grad_gate = grad_gated * mixed * sigmoid_gate * (1.0 + gate * (1.0 - sigmoid_gate))

    def state_effect(carried_in):
        return finish(kept, carried_in, skip_weight)

    ignored, state_pull = jax.vjp(state_effect, carried)
    (through_mixed,) = state_pull(grad_mixed)
    later_decay, next_grad = prefix(
        (final_product, through_mixed), "ctx", chain_backward, identity, True
    )

    def full_mixer(padded_in, raw_in, weight_in, bias_in, step_in, decay_in, skip_in, carried_in):
        return mixer(
            padded_in,
            flags_padded,
            sequence_starts,
            raw_in,
            weight_in,
            bias_in,
            step_in,
            decay_in,
            skip_in,
            carried_in,
        )

    ignored_out, pullback = jax.vjp(
        full_mixer,
        padded,
        step_raw,
        conv_weight,
        conv_bias,
        step_bias,
        decay_log,
        skip_weight,
        carried,
    )
    (
        grad_padded,
        grad_step_raw,
        grad_conv_weight,
        grad_conv_bias,
        grad_step_bias,
        grad_decay_log,
        grad_skip,
        grad_carried,
    ) = pullback((grad_mixed, next_grad))
    returned = passed_along(grad_padded[:width], "ctx", -1)
    grad_rows = grad_padded[width:]
    grad_rows = grad_rows.at[-width:].add(returned)
    shared_rows, shared_weight, shared_bias = lax.psum(
        (
            grad_rows[:, local_inner:],
            grad_conv_weight[:, local_inner:],
            grad_conv_bias[local_inner:],
        ),
        "tp",
    )
    grad_main = jnp.concatenate(
        [grad_gate, grad_rows[:, :local_inner], shared_rows], axis=1
    ).astype(jnp.bfloat16)
    grad_step = grad_step_raw.astype(jnp.bfloat16)
    grad_main_weight = jnp.dot(normed.T, grad_main, preferred_element_type=jnp.float32)
    grad_step_weight = jnp.dot(normed.T, grad_step, preferred_element_type=jnp.float32)
    tensor_part = jnp.dot(
        grad_main[:, : 2 * local_inner],
        main_weight[:, : 2 * local_inner].T,
        preferred_element_type=jnp.float32,
    )
    tensor_part = tensor_part + jnp.dot(grad_step, full_step.T, preferred_element_type=jnp.float32)
    own_cotangent = lax.dynamic_slice_in_dim(output_cotangent, column, share, 1).astype(jnp.float32)
    shared_part = jnp.dot(
        grad_main[:, 2 * local_inner :], full_state.T, preferred_element_type=jnp.float32
    )
    grad_normed = lax.psum(tensor_part, "tp") + shared_part
    scaled_in = grad_normed * norm_gain[None, :]
    mean_term = jnp.mean(hidden * scaled_in, axis=1, keepdims=True)
    own_grad = lax.dynamic_slice_in_dim(grad_normed, column, share, 1)
    own_scaled = lax.dynamic_slice_in_dim(scaled_in, column, share, 1)
    input_grad = own_cotangent + inv_rms * own_scaled - own_hidden * inv_rms**3 * mean_term
    grad_gain_norm = jnp.sum(own_grad * own_hidden * inv_rms, axis=0)
    gate_grad, input_proj_grad, step_proj_grad, state_grad, out_proj_grad = (
        lax.psum_scatter(
            grad_main_weight[:, :local_inner], ("dp", "ctx"), scatter_dimension=0, tiled=True
        ),
        lax.psum_scatter(
            grad_main_weight[:, local_inner : 2 * local_inner],
            ("dp", "ctx"),
            scatter_dimension=0,
            tiled=True,
        ),
        lax.psum_scatter(grad_step_weight, ("dp", "ctx"), scatter_dimension=0, tiled=True),
        lax.psum_scatter(
            grad_main_weight[:, 2 * local_inner :], ("dp", "ctx"), scatter_dimension=0, tiled=True
        ),
        lax.psum_scatter(grad_out, ("dp", "ctx"), scatter_dimension=1, tiled=True),
    )
    smalls = lax.psum(
        (
            grad_conv_weight[:, :local_inner],
            grad_conv_bias[:local_inner],
            shared_weight,
            shared_bias,
            grad_step_bias,
            grad_decay_log,
            grad_skip,
            grad_gain_gate,
            grad_gain_norm,
        ),
        ("dp", "ctx"),
    )
    return (
        block_output,
        input_grad,
        smalls[8],
        gate_grad,
        input_proj_grad,
        step_proj_grad,
        state_grad,
        smalls[0],
        smalls[1],
        smalls[2],
        smalls[3],
        smalls[4],
        smalls[5],
        smalls[6],
        smalls[7],
        out_proj_grad,
    )


def solution(mesh):
    return jax.shard_map(
        on_device,
        mesh=mesh,
        in_specs=(
            P(("dp", "ctx"), None),
            P(("dp", "ctx")),
            P(),
            P(("dp", "ctx"), "tp"),
            P(("dp", "ctx"), "tp"),
            P(("dp", "ctx"), "tp"),
            P(("dp", "ctx"), None),
            P(None, "tp"),
            P("tp"),
            P(),
            P(),
            P("tp"),
            P("tp"),
            P("tp"),
            P("tp"),
            P("tp", ("dp", "ctx")),
            P(("dp", "ctx"), None),
        ),
        out_specs=(
            P(("dp", "ctx"), "tp"),
            P(("dp", "ctx"), "tp"),
            P("tp"),
            P(("dp", "ctx"), "tp"),
            P(("dp", "ctx"), "tp"),
            P(("dp", "ctx"), "tp"),
            P(("dp", "ctx"), None),
            P(None, "tp"),
            P("tp"),
            P(),
            P(),
            P("tp"),
            P("tp"),
            P("tp"),
            P("tp"),
            P("tp", ("dp", "ctx")),
        ),
        check_vma=False,
    )
```

profile of v0, /device:TPU:0, one launch (start us, length us, event | category | flops | bytes accessed | tf_op | source)
XLA Modules:
  0.0 829.4 jit_solution(5136815848027161430)
XLA Ops:
  9.5 2.4 collective-permute-start.1
  13.9 2.1 multiply_reduce_fusion.2
  16.7 10.0 %all_gather.36 = bf16[1024,8]{0,1:T(8,128)(2,1)S(1)} all-gather(bf16[128,8]{0,1:T(8,128)(2,1)} %param.34), channel_id=1, replica_groups=mesh['dp'=4,'ctx'=2,'tp'=4] {'dp','ctx'}, dimensions={0}, use_global_device_ids=true | all-gather | bytes 18432 | tf_op jit(solution)/shard_map/all_gather | solution.py:184
  27.4 3.0 compare_select_fusion.2
  30.4 2.3 reduce-window.35
  32.8 9.7 %all_gather.35 = bf16[1024,256]{1,0:T(8,128)(2,1)S(1)} all-gather(bf16[128,256]{1,0:T(8,128)(2,1)S(1)} %copy-done.37), channel_id=1, replica_groups=mesh['dp'=4,'ctx'=2,'tp'=4] {'dp','ctx'}, dimensions={0}, use_global_device_ids=true | all-gather | bytes 589824 | tf_op jit(solution)/shard_map/all_gather | solution.py:185
  48.4 13.0 %all-gather.9.cloned.1.call-done = bf16[1024,512]{1,0:T(8,128)(2,1)} async-done(((bf16[128,512]{1,0:T(8,128)(2,1)}), bf16[1024,512]{1,0:T(8,128)(2,1)}) %all-gather.9.cloned.1.call-update) | async-done | bytes 1048592 | tf_op jit(solution)/shard_map/all_gather | solution.py:183
  61.4 6.8 fusion.128
  68.2 2.1 collective-permute-start
  71.6 4.0 fusion.40
  79.0 4.4 reshape.384
  83.4 3.8 copy.144
  87.2 4.6 fusion.67
  93.5 17.3 %while.86 = (s32[]{:T(128)}, f32[8,64,128]{2,1,0:T(8,128)S(1)}, f32[8]{0:T(128)}, f32[4,8,64,128]{3,2,1,0:T(8,128)}, f32[4,8]{1,0:T(4,128)}, /*index=5*/f32[4,8]...) while((s32[]{:T(128)}, f32[8,64,128]{2,1,0:T(8,128)S(1)}, f32[8]{0:T(128)}, ...), condition=%wide.region_8.9_spmd.clone, body=%wide.region_7.8_spmd.clone.sunk | while | flops 262163 | bytes 1311605 | solution.py:92
  110.8 2.3 all-gather.1
  114.0 2.5 all-reduce.14
  117.4 2.3 fusion.129
  119.8 3.6 fusion.82
  123.4 11.1 %fusion.60 = f32[4,256,8,64]{1,3,2,0:T(8,128)} fusion(f32[4,256,8,64]{1,3,2,0:T(8,128)S(1)} %copy-done.7, f32[4,256,8,64]{1,3,2,0:T(8,128)S(1)} %fusion.82, f32[4,256,8]{1,2,0:T(8,128)S(1)} %bitcast.228, f32[4,256,256]{2,1,0:T(8,128)S(1)} %fusion.129, f32[4,256,8]{1,2,0:T(8,128)S(1)} %get-tuple-element.635, pred[4,256,256]{2,1,0:T(8,128)(4,1)S(1)} %copy-done.35, ...), kind=kOutput, calls=%fused_computation.103 | convolution fusion | flops 1623195648 | bytes 7700512 | tf_op jit(solution)/shard_map/ktsh,kshp->kthp/dot_general | solution.py:73
  134.5 3.9 copy.173
  138.4 4.8 reshape.385
  143.2 4.2 multiply_reduce_fusion.12
  147.4 12.2 %psum.105 = f32[1024]{0:T(1024)} all-reduce(f32[1024]{0:T(1024)S(1)} %get-tuple-element.632), channel_id=1, replica_groups=mesh['dp'=4,'ctx'=2,'tp'=4] {'tp'}, use_global_device_ids=true, to_apply=%region_12.13 | all-reduce | flops 1024 | bytes 8192 | tf_op jit(solution)/shard_map/psum | solution.py:224
  160.9 5.9 multiply_reduce_fusion.7
  166.9 9.5 %psum.106 = f32[1024]{0:T(1024)} all-reduce(f32[1024]{0:T(1024)} %get-tuple-element.529), channel_id=1, replica_groups=mesh['dp'=4,'ctx'=2,'tp'=4] {'tp'}, use_global_device_ids=true, to_apply=%region_15.16 | all-reduce | flops 1024 | bytes 8192 | tf_op jit(solution)/shard_map/psum | solution.py:240
  177.0 6.6 multiply_reduce_fusion.8
  183.6 2.9 copy.151
  186.5 3.2 reshape.357
  191.3 28.2 %while.87 = (s32[]{:T(128)}, f32[8,64,128]{2,1,0:T(8,128)}, f32[8]{0:T(128)}, f32[4,8,64,128]{3,2,1,0:T(8,128)}, f32[4,8]{1,0:T(4,128)}, /*index=5*/f32[4,8,1,1]...) while((s32[]{:T(128)}, f32[8,64,128]{2,1,0:T(8,128)}, ...), condition=%wide.region_17.18_spmd.clone, body=%wide.region_16.17_spmd.clone.sunk | while | flops 262163 | bytes 1313149 | solution.py:92
  219.5 5.5 multiply_reduce_fusion.14
  225.0 2.3 all-gather.2
  230.7 6.4 fusion.77
  238.2 15.5 %while.85 = (s32[]{:T(128)}, f32[8,64,128]{2,1,0:T(8,128)S(1)}, f32[8]{0:T(128)}, f32[4,8,64,128]{3,2,1,0:T(8,128)}, f32[4,8]{1,0:T(4,128)S(1)}, /*index=5*/f32[...) while((s32[]{:T(128)}, f32[8,64,128]{2,1,0:T(8,128)S(1)}, ...), condition=%wide.region_26.27_spmd, body=%wide.region_24.26_spmd.sunk | while | flops 262171 | bytes 1573445 | solution.py:92
  254.2 5.6 fusion.78
  262.0 14.2 %fusion.25 = (f32[4,256,8]{1,2,0:T(8,128)S(1)}, f32[4,256,8]{1,2,0:T(8,128)S(1)}, f32[4,256,8]{1,2,0:T(8,128)S(1)}, f32[4,256,256]{2,1,0:T(8,128)S(1)}) fusion(f32[4,256,8]{1,2,0:T(8,128)S(1)} %bitcast.229, f32[4,256,256]{2,1,0:T(8,128)S(1)} %copy-done.29, f32[4,256,8]{1,2,0:T(8,128)S(1)} %get-tuple-element.635, pred[4,256,256]{2,1,0:T(8,128)(4,1)S(1)} %copy-done.36, ...), kind=kOutput, calls=%fused_computation.49 | convolution fusion | flops 1641783296 | bytes 6717440 | tf_op jit(solution)/shard_map/transpose(jvp(ktsh,kshp->kthp))/dot_general | solution.py:73
  278.0 2.7 convolution_add_fusion.2
  280.7 9.1 %bitcast_add_fusion.5 = f32[4,256,8,64]{1,3,2,0:T(8,128)} fusion(f32[4,256,8,64]{1,3,2,0:T(8,128)S(1)} %get-tuple-element.679, f32[4,256,8]{1,2,0:T(8,128)S(1)} %bitcast.230, f32[4,256,256]{2,1,0:T(8,128)S(1)} %copy-done.29, f32[4,256,8]{1,2,0:T(8,128)S(1)} %get-tuple-element.635, pred[4,256,256]{2,1,0:T(8,128)(4,1)S(1)} %copy-done.36, ...), kind=kOutput, calls=%fused_computation.101 | convolution fusion | flops 1622147072 | bytes 7700480 | tf_op jit(solution)/shard_map/transpose(jvp(ktsh,kshp->kthp))/dot_general | solution.py:73
  289.8 3.9 copy.170
  293.7 4.8 reshape.383
  298.5 2.9 multiply_add_fusion.1
  301.9 4.4 multiply_reduce_fusion.6
  311.2 2.6 pad_add_fusion
  317.8 10.2 %reduce-window.39 = f32[4,8,2,128]{3,1,2,0:T(8,128)S(1)} reduce-window(f32[4,8,2,128]{3,1,2,0:T(8,128)S(1)} %get-tuple-element.656, f32[]{:T(128)} %constant.206.clone.1), window={size=1x1x1x128 pad=0_0x0_0x0_0x0_127}, to_apply=%region_33.34 | reduce-window | flops 1040384 | bytes 65540 | tf_op jit(solution)/shard_map/reduce-window.6
  328.4 3.9 slice.261
  337.2 4.6 fusion.53
  341.8 2.8 convolution_add_fusion
  346.4 3.3 fusion.118
  350.5 3.0 fusion.100
  354.9 82.4 %all-reduce.21 = (bf16[1024,256]{1,0:T(8,128)(2,1)}, f32[4,256]{1,0:T(4,128)S(1)}, f32[256]{0:T(256)S(1)}) all-reduce(f32[1024,256]{1,0:T(8,128)S(1)} %slice.265, f32[4,256]{1,0:T(4,128)S(1)} %pad_add_fusion.3, f32[256]{0:T(256)S(1)} %slice.234), channel_id=1, replica_groups=mesh['dp'=4,'ctx'=2,'tp'=4] {'tp'}, use_global_device_ids=true, to_apply=%region_36.37 | all-reduce | flops 263424 | bytes 1583104 | tf_op jit(solution)/shard_map/psum | solution.py:294
  437.3 5.4 fusion.47
  442.7 2.4 copy-done.21
  446.2 4.3 fusion.117
  450.5 4.7 fusion.126
  456.9 2.5 convert_element_type.46
  459.6 74.6 %all-reduce.20.cloned.1.call-done = f32[1024,1024]{1,0:T(8,128)} async-done(((f32[1024,1024]{1,0:T(8,128)}), f32[1024,1024]{1,0:T(8,128)}) %all-reduce.20.cloned.1.call-update) | async-done | bytes 4194320 | tf_op jit(solution)/shard_map/psum | solution.py:318
  534.2 6.4 multiply_reduce_fusion.1
  540.7 71.5 %reduce-scatter.7.cloned.1.call-done = f32[1024,256]{1,0:T(8,128)} async-done(((f32[1024,1024]{1,0:T(8,128)}), f32[1024,256]{1,0:T(8,128)}) %reduce-scatter.7.cloned.1.call-update) | async-done | bytes 1048592 | tf_op jit(solution)/shard_map/reduce_scatter | solution.py:229
  612.2 3.9 multiply_reduce_fusion.13
  616.1 24.3 %all-reduce.15 = (f32[256]{0:T(256)}, f32[4,512]{1,0:T(4,128)}, f32[512]{0:T(512)}, f32[4,256]{1,0:T(4,128)}, f32[256]{0:T(256)}, /*index=5*/f32[8]{0:T(128)}, f32[8]{0:T(128)}, f32[8]{0:T(128)}, f32[512]{0:T(512)}) all-reduce(f32[256]{0:T(256)S(1)} %get-tuple-element.647, ...), channel_id=1, replica_groups=mesh['dp'=4,'ctx'=2,'tp'=4] {'dp','ctx'}, use_global_device_ids=true, to_apply=%region_39.40 | all-reduce | flops 4632 | bytes 37056 | tf_op jit(solution)/shard_map/psum | solution.py:341
  640.5 7.0 reduce-scatter.13.cloned.1.call-done
  647.4 39.7 %reduce-scatter.15.cloned.1.call-done = f32[128,256]{1,0:T(8,128)} async-done(((f32[1024,256]{1,0:T(8,128)}), f32[128,256]{1,0:T(8,128)}) %reduce-scatter.15.cloned.1.call-update) | async-done | bytes 131088 | tf_op jit(solution)/shard_map/reduce_scatter | solution.py:336
  687.2 45.0 %reduce-scatter.17.cloned.1.call-done = f32[512,128]{1,0:T(8,128)} async-done(((f32[512,1024]{1,0:T(8,128)}), f32[512,128]{1,0:T(8,128)}) %reduce-scatter.17.cloned.1.call-update) | async-done | bytes 262160 | tf_op jit(solution)/shard_map/reduce_scatter | solution.py:339
  732.2 45.0 %reduce-scatter.11.cloned.1.call-done = f32[128,512]{1,0:T(8,128)} async-done(((f32[1024,512]{1,0:T(8,128)}), f32[128,512]{1,0:T(8,128)}) %reduce-scatter.11.cloned.1.call-update) | async-done | bytes 262160 | tf_op jit(solution)/shard_map/reduce_scatter | solution.py:329
  777.2 44.8 %reduce-scatter.9.cloned.1.call-done = f32[128,512]{1,0:T(8,128)} async-done(((f32[1024,512]{1,0:T(8,128)}), f32[128,512]{1,0:T(8,128)}) %reduce-scatter.9.cloned.1.call-update) | async-done | bytes 262160 | tf_op jit(solution)/shard_map/reduce_scatter | solution.py:326
  (364 shorter events, 115.6 us)
Async XLA Ops:
  7.2 41.3 %all-gather.7.cloned.1.call-start = ((), (), s32[]{:S(2)}) async-start(), calls=%async_computation.6 | async-start | bytes 1179648 | tf_op jit(solution)/shard_map/all_gather | solution.py:182
  7.9 53.5 %all-gather.9.cloned.1.call-start = ((), (), s32[]{:S(2)}) async-start(), calls=%async_computation.7 | async-start | bytes 1179648 | tf_op jit(solution)/shard_map/all_gather | solution.py:183
  8.7 152.3 %all-gather.11.cloned.1.call-start = ((), (), s32[]{:S(2)}) async-start(), calls=%async_computation.8 | async-start | bytes 1179648 | tf_op jit(solution)/shard_map/all_gather | solution.py:186
  9.5 38.2 %collective-permute-start.1 = (bf16[3]{0:T(256)(128)(2,1)S(1)}, bf16[3]{0:T(256)(128)(2,1)S(1)}, u32[]{:S(2)}, u32[]{:S(2)}) collective-permute-start(bf16[3]{0:T(256)(128)(2,1)S(1)} %slice.193), channel_id=1, source_target_pairs={{0,4},{1,5},{2,6},{3,7},{8,12},{9,13},{10,14},{11,15},{16,20},{17,... | collective-permute-start | bytes 26 | tf_op jit(solution)/shard_map/ppermute | solution.py:21
  11.9 522.3 %all-reduce.20.cloned.1.call-start = ((), (), s32[]{:S(2)}) async-start(), calls=%async_computation.10 | async-start | bytes 8388608 | tf_op jit(solution)/shard_map/psum | solution.py:318
  13.9 31.0 %copy-start.69 = (pred[4,256]{1,0:T(4,128)(4,1)}, pred[4,256]{1,0:T(4,128)(4,1)S(1)}, u32[]{:S(2)}) copy-start(pred[4,256]{1,0:T(4,128)(4,1)S(1)} %get-tuple-element.670) | copy-start | bytes 3076
  13.9 33.7 %copy-start.66 = (pred[4,256]{1,0:T(4,128)(4,1)}, pred[4,256]{1,0:T(4,128)(4,1)S(1)}, u32[]{:S(2)}) copy-start(pred[4,256]{1,0:T(4,128)(4,1)S(1)} %get-tuple-element.669) | copy-start | bytes 3076
  13.9 18.9 %copy-start.37 = (bf16[128,256]{1,0:T(8,128)(2,1)S(1)}, bf16[128,256]{1,0:T(8,128)(2,1)}, u32[]{:S(2)}) copy-start(bf16[128,256]{1,0:T(8,128)(2,1)} %param.35) | copy-start | bytes 196612
  13.9 28.6 %copy-start.75 = (f32[4,512]{1,0:T(4,128)S(1)}, f32[4,512]{1,0:T(4,128)}, u32[]{:S(2)}) copy-start(f32[4,512]{1,0:T(4,128)} %param.36) | copy-start | bytes 24580
  13.9 28.6 %copy-start.79 = (f32[4,256]{1,0:T(4,128)S(1)}, f32[4,256]{1,0:T(4,128)}, u32[]{:S(2)}) copy-start(f32[4,256]{1,0:T(4,128)} %param.38) | copy-start | bytes 12292
  13.9 30.3 %copy-start.85 = (f32[8]{0:T(128)S(1)}, f32[8]{0:T(128)}, u32[]{:S(2)}) copy-start(f32[8]{0:T(128)} %param.42) | copy-start | bytes 100
  16.1 29.7 %copy-start.80 = (f32[512]{0:T(512)S(1)}, f32[512]{0:T(512)}, u32[]{:S(2)}) copy-start(f32[512]{0:T(512)} %param.37) | copy-start | bytes 6148
  16.1 29.7 %copy-start.82 = (f32[256]{0:T(256)S(1)}, f32[256]{0:T(256)}, u32[]{:S(2)}) copy-start(f32[256]{0:T(256)} %param.39) | copy-start | bytes 3076
  16.1 30.3 %copy-start.88 = (u32[32]{0:T(128)S(1)}, u32[32]{0:T(128)}, u32[]{:S(2)}) copy-start(u32[32]{0:T(128)} %constant.246) | copy-start | bytes 388
  16.1 45.3 %copy-start.14 = (bf16[1024,1024]{1,0:T(8,128)(2,1)S(1)}, bf16[1024,1024]{1,0:T(8,128)(2,1)}, u32[]{:S(2)}) copy-start(bf16[1024,1024]{1,0:T(8,128)(2,1)} %param.29) | copy-start | bytes 6291460
  16.1 45.3 %copy-start.77 = (f32[1024]{0:T(1024)S(1)}, f32[1024]{0:T(1024)}, u32[]{:S(2)}) copy-start(f32[1024]{0:T(1024)} %param.31) | copy-start | bytes 12292
  16.7 51.5 %copy-start.60 = (f32[1024]{0:T(1024)}, f32[1024]{0:T(1024)S(1)}, u32[]{:S(2)}) copy-start(f32[1024]{0:T(1024)S(1)} %get-tuple-element.666) | copy-start | bytes 12292
  27.4 5.3 copy-start.83
  30.4 37.9 %copy-start.32 = (f32[1024,8]{0,1:T(8,128)}, f32[1024,8]{0,1:T(8,128)S(1)}, u32[]{:S(2)}) copy-start(f32[1024,8]{0,1:T(8,128)S(1)} %get-tuple-element.659) | copy-start | bytes 98308
  42.5 25.7 %copy-start.25 = (bf16[1024,256]{1,0:T(8,128)(2,1)}, bf16[1024,256]{1,0:T(8,128)(2,1)S(1)}, u32[]{:S(2)}) copy-start(bf16[1024,256]{1,0:T(8,128)(2,1)S(1)} %all_gather.35) | copy-start | bytes 1572868
  68.2 3.0 collective-permute-start
  117.3 102.2 %copy-start.9 = (f32[8,64,128]{2,1,0:T(8,128)}, f32[8,64,128]{2,1,0:T(8,128)S(1)}, u32[]{:S(2)}) copy-start(f32[8,64,128]{2,1,0:T(8,128)S(1)} %get-tuple-element.462) | copy-start | bytes 786436
  117.3 6.0 copy-start.7
  117.4 6.0 copy-start.33
  117.4 6.0 copy-start.35
  117.4 6.0 copy-start.86
  119.7 3.6 copy-start.28
  253.7 6.2 copy-start.8
  253.7 6.2 copy-start.18
  253.7 6.2 copy-start.20
  262.0 14.2 %copy-start.22 = (f32[4,256,128]{2,1,0:T(8,128)S(1)}, f32[4,256,128]{2,1,0:T(8,128)}, u32[]{:S(2)}) copy-start(f32[4,256,128]{2,1,0:T(8,128)} %fusion.77) | copy-start | bytes 1572868
  262.0 16.1 %copy-start.16 = (f32[1024,128]{1,0:T(8,128)S(1)}, f32[1024,128]{1,0:T(8,128)}, u32[]{:S(2)}) copy-start(f32[1024,128]{1,0:T(8,128)} %get-tuple-element.655) | copy-start | bytes 1572868
  293.7 4.8 copy-start.72
  298.5 3.4 copy-start.24
  298.5 3.4 copy-start.39
  301.9 4.4 copy-start.46
  301.9 4.4 copy-start.48
  301.9 4.4 copy-start.50
  301.9 4.4 copy-start.52
  307.6 3.6 copy-start.4
  313.8 3.5 copy-start.56
  313.9 3.5 copy-start.67
  313.9 3.7 copy-start.74
  313.9 3.8 copy-start.70
  313.9 14.3 %copy-start.54 = (f32[1024,8]{0,1:T(8,128)S(1)}, f32[1024,8]{0,1:T(8,128)}, u32[]{:S(2)}) copy-start(f32[1024,8]{0,1:T(8,128)} %get-tuple-element.675) | copy-start | bytes 98308
  313.9 14.3 %copy-start.84 = (f32[8]{0:T(128)S(1)}, f32[8]{0:T(128)}, u32[]{:S(2)}) copy-start(f32[8]{0:T(128)} %copy-done.83) | copy-start | bytes 100
  316.0 16.3 %collective-permute-start.2 = (f32[3,768]{1,0:T(4,128)}, f32[3,768]{1,0:T(4,128)}, u32[]{:S(2)}, u32[]{:S(2)}) collective-permute-start(f32[3,768]{1,0:T(4,128)} %pad_add_fusion.1), channel_id=1, source_target_pairs={{4,0},{5,1},{6,2},{7,3},{12,8},{13,9},{14,10},{15,11},{20,16},{21,... | collective-permute-start | bytes 27656 | tf_op jit(solution)/shard_map/ppermute | solution.py:21
  328.4 4.0 copy-start.1
  328.4 4.9 copy-start.3
  337.2 4.6 copy-start.30
  344.6 267.6 %reduce-scatter.7.cloned.1.call-start = ((), (), s32[]{:S(2)}) async-start(), calls=%async_computation.9 | async-start | bytes 5242880 | tf_op jit(solution)/shard_map/reduce_scatter | solution.py:229
  349.7 297.7 %reduce-scatter.13.cloned.1.call-start = ((), (), s32[]{:S(2)}) async-start(), calls=%async_computation.13 | async-start | bytes 36864 | tf_op jit(solution)/shard_map/reduce_scatter | solution.py:335
  353.5 333.6 %reduce-scatter.15.cloned.1.call-start = ((), (), s32[]{:S(2)}) async-start(), calls=%async_computation.14 | async-start | bytes 1179648 | tf_op jit(solution)/shard_map/reduce_scatter | solution.py:336
  446.1 286.1 %reduce-scatter.17.cloned.1.call-start = ((), (), s32[]{:S(2)}) async-start(), calls=%async_computation.15 | async-start | bytes 2359296 | tf_op jit(solution)/shard_map/reduce_scatter | solution.py:339
  450.5 326.7 %reduce-scatter.11.cloned.1.call-start = ((), (), s32[]{:S(2)}) async-start(), calls=%async_computation.12 | async-start | bytes 2359296 | tf_op jit(solution)/shard_map/reduce_scatter | solution.py:329
  455.3 366.7 %reduce-scatter.9.cloned.1.call-start = ((), (), s32[]{:S(2)}) async-start(), calls=%async_computation.11 | async-start | bytes 2359296 | tf_op jit(solution)/shard_map/reduce_scatter | solution.py:326
  456.9 77.4 %copy-start.26 = (bf16[1024,256]{1,0:T(8,128)(2,1)S(1)}, bf16[1024,256]{1,0:T(8,128)(2,1)}, u32[]{:S(2)}) copy-start(bf16[1024,256]{1,0:T(8,128)(2,1)} %copy-done.25) | copy-start | bytes 1572868
  456.9 77.4 %copy-start.31 = (bf16[1024,256]{1,0:T(8,128)(2,1)S(1)}, bf16[1024,256]{1,0:T(8,128)(2,1)}, u32[]{:S(2)}) copy-start(bf16[1024,256]{1,0:T(8,128)(2,1)} %get-tuple-element.618) | copy-start | bytes 1572868
  459.4 81.3 %copy-start.71 = (f32[1,768]{1,0:T(1,128)}, f32[1,768]{1,0:T(1,128)S(1)}, u32[]{:S(2)}) copy-start(f32[1,768]{1,0:T(1,128)S(1)} %reshape.370) | copy-start | bytes 9220
  459.4 81.3 %copy-start.53 = (f32[4,768]{1,0:T(4,128)}, f32[4,768]{1,0:T(4,128)S(1)}, u32[]{:S(2)}) copy-start(f32[4,768]{1,0:T(4,128)S(1)} %pad_add_fusion.2) | copy-start | bytes 36868
  459.6 152.5 %copy-start.59 = (f32[1024]{0:T(1024)S(1)}, f32[1024]{0:T(1024)}, u32[]{:S(2)}) copy-start(f32[1024]{0:T(1024)} %get-tuple-element.665) | copy-start | bytes 12292
  612.2 3.9 slice-start
  612.2 3.9 slice-start.1
  612.2 3.9 copy-start.81
  (40 other events, 73.7 us)
Sparse Core Ops, SparseCore 0:
  9.9 26.1 all-gather.6
  37.9 23.4 all-gather.8
  63.3 23.4 all-gather.10
  344.7 189.4 all-reduce.19
  536.4 75.7 reduce-scatter.6
  615.6 31.7 reduce-scatter.12
  651.2 35.9 reduce-scatter.14
  691.0 41.1 reduce-scatter.16
  736.0 41.0 reduce-scatter.10
  780.9 41.0 reduce-scatter.8
where the time goes:
time: 840 us; the launch traced here: 829 us
  waiting for transfers between devices  343 us (41%)
  blocking collectives  155 us (18%)
  matrix products  116 us (14%)
  other arithmetic  99.7 us (12%)
  local copies, waits for them, and re-layouts  91.8 us (11%)
  between operations  16.4 us (2%)
    psum x1, blocking collectives, on_device(): lax.psum((grad_rows[:, local_inner:], grad_conv_weight[:, local_inner:],...  82.4 us
    psum x1, waiting for transfers between devices, on_device(): grad_normed = lax.psum(tensor_part, 'tp') + shared_part  74.6 us
    reduce_scatter x1, waiting for transfers between devices, on_device(): lax.psum_scatter(jnp.dot(gated_normed, full_out, preferred_element_type=j...  71.5 us
    reduce_scatter x1, waiting for transfers between devices, on_device(): lax.psum_scatter(grad_out, ('dp', 'ctx'), scatter_dimension=1, tiled=True)  45 us
    reduce_scatter x1, waiting for transfers between devices, on_device(): lax.psum_scatter(grad_main_weight[:, local_inner:2 * local_inner], ('dp',...  45 us
    reduce_scatter x1, waiting for transfers between devices, on_device(): lax.psum_scatter(grad_main_weight[:, :local_inner], ('dp', 'ctx'), scatte...  44.8 us
    reduce_scatter x1, waiting for transfers between devices, on_device(): lax.psum_scatter(grad_main_weight[:, 2 * local_inner:], ('dp', 'ctx'), sc...  39.7 us
    dot_general x3, matrix products, span_parts(): jnp.einsum('ktsh,kshp->kthp', mixing, block_values, precision=HIGHEST)  34.3 us
  transfers between devices with their start and end apart: 13, of which 9 were waited for; matrix products, arithmetic and copies ran while one was open for 18% of the time, Pallas kernels for 0%

commit v1 on v0

v1 whole, which is shorter than its diff:
```python
import jax
import jax.numpy as jnp
from jax import lax
from jax.sharding import PartitionSpec as P

MODEL_WIDTH = 1024
HEADDIM = 64
STATE = 128
KCONV = 4
SPAN = 256
INNER = 2048


EPSILON = 1e-05
HIGHEST = lax.Precision.HIGHEST


def passed_along(block, distance):
    devices = range(lax.axis_size("ctx"))
    route = [(i - distance, i) for i in devices if i - distance in devices]
    return lax.ppermute(block, "ctx", route)


def conv_apply(padded, flags_padded, conv_weight, conv_bias):
    width = KCONV - 1
    count = padded.shape[0] - width
    segments = jnp.cumsum(flags_padded)
    own = segments[width:]
    result = jnp.zeros((count, padded.shape[1]), jnp.float32) + conv_bias[None, :]
    for lag in range(KCONV):
        valid = (segments[width - lag : width - lag + count] == own).astype(jnp.float32)
        result = (
            result
            + conv_weight[lag][None, :] * padded[width - lag : width - lag + count] * valid[:, None]
        )
    return result


def span_parts(inner_values, step_size, state_in, state_out, sequence_starts, decay_rate):
    count = inner_values.shape[0]
    heads = step_size.shape[1]
    spans = count // SPAN
    log_decay = (step_size * decay_rate[None, :]).reshape(spans, SPAN, heads)
    ones_below = jnp.tril(jnp.ones((SPAN, SPAN), jnp.float32))
    cumulative = jnp.einsum("ts,ksh->kth", ones_below, log_decay, precision=HIGHEST)
    segments = jnp.cumsum(sequence_starts.reshape(spans, SPAN), axis=1)
    block_values = inner_values.reshape(spans, SPAN, heads, HEADDIM)
    block_step = step_size.reshape(spans, SPAN, heads)
    block_in = state_in.reshape(spans, SPAN, STATE)
    block_out = state_out.reshape(spans, SPAN, STATE)
    order = jnp.arange(SPAN)
    lower = order[:, None] >= order[None, :]
    same = ((segments[:, :, None] == segments[:, None, :]) & lower[None])[..., None]
    spread = cumulative[:, :, None, :] - cumulative[:, None, :, :]
    decay = jnp.where(same, jnp.exp(jnp.where(same, spread, 0.0)), 0.0)
    scores = jnp.einsum("ktn,ksn->kts", block_out, block_in)
    mixing = decay * scores[..., None] * block_step[:, None, :, :]
    inner_mixed = jnp.einsum("ktsh,kshp->kthp", mixing, block_values)
    ending = (segments == segments[:, -1:])[..., None]
    to_end = jnp.where(ending, jnp.exp(cumulative[:, -1:, :] - cumulative), 0.0) * block_step
    states = jnp.einsum(
        "kshp,ksn->khpn", block_values * to_end[..., None], block_in
    )
    passing = jnp.where((segments == 0)[..., None], jnp.exp(cumulative), 0.0)
    return (inner_mixed, states, passing)


def fold_spans(states, passing):
    ends = passing[:, -1, :]
    state = jnp.zeros(states.shape[1:], jnp.float32)
    product = jnp.ones(ends.shape[1:], jnp.float32)
    span_states, span_decays = [], []
    for k in range(states.shape[0]):
        span_states.append(state)
        span_decays.append(product)
        state = ends[k][:, None, None] * state + states[k]
        product = ends[k] * product
    return (jnp.stack(span_states), jnp.stack(span_decays), state, product)


def mixer_front(
    padded, flags_padded, sequence_starts, step_raw, conv_weight, conv_bias, step_bias, decay_log
):
    inner_width = padded.shape[1] - 2 * STATE
    activated = jax.nn.silu(conv_apply(padded, flags_padded, conv_weight, conv_bias))
    inner_values = activated[:, :inner_width]
    state_in = activated[:, inner_width : inner_width + STATE]
    state_out = activated[:, inner_width + STATE :]
    step_size = jax.nn.softplus(step_raw + step_bias[None, :])
    decay_rate = -jnp.exp(decay_log)
    inner_mixed, states, passing = span_parts(
        inner_values, step_size, state_in, state_out, sequence_starts, decay_rate
    )
    span_states, span_decays, final_state, final_product = fold_spans(states, passing)
    kept = (inner_values, state_out, inner_mixed, passing, span_states, span_decays)
    return (kept, final_state, final_product)


def finish(kept, carried, skip):
    inner_values, state_out, inner_mixed, passing, span_states, span_decays = kept
    spans = inner_mixed.shape[0]
    heads = inner_mixed.shape[2]
    initial = span_states + span_decays[:, :, None, None] * carried[None]
    block_out = state_out.reshape(spans, SPAN, STATE)
    from_state = jnp.einsum("ktn,khpn->kthp", block_out, initial)
    block_values = inner_values.reshape(spans, SPAN, heads, HEADDIM)
    total = inner_mixed + passing[..., None] * from_state + skip[None, None, :, None] * block_values
    return total.reshape(inner_values.shape[0], heads * HEADDIM)


def mixer(
    padded,
    flags_padded,
    sequence_starts,
    step_raw,
    conv_weight,
    conv_bias,
    step_bias,
    decay_log,
    skip,
    carried,
):
    kept, final_state, final_product = mixer_front(
        padded,
        flags_padded,
        sequence_starts,
        step_raw,
        conv_weight,
        conv_bias,
        step_bias,
        decay_log,
    )
    output = finish(kept, carried, skip)
    return (output, final_state + final_product[:, None, None] * carried)


def on_device(
    block_input_activations,
    sequence_first_token,
    norm_gain,
    gate_proj,
    input_proj,
    step_proj,
    state_proj,
    conv_inner_weight,
    conv_inner_bias,
    conv_state_weight,
    conv_state_bias,
    step_bias,
    decay_log,
    skip_weight,
    gate_gain,
    out_proj,
    output_cotangent,
):
    everyone = ("dp", "ctx")
    bf16 = jnp.bfloat16
    local_inner = gate_proj.shape[1]
    heads = step_bias.shape[0]
    width = KCONV - 1
    full_weight = lax.all_gather(
        jnp.concatenate([gate_proj, input_proj, state_proj, step_proj], axis=1),
        everyone,
        axis=0,
        tiled=True,
    )
    full_out_t = lax.all_gather(out_proj.T, everyone, axis=0, tiled=True)
    hidden = block_input_activations.astype(jnp.float32)
    inv_rms = lax.rsqrt(jnp.mean(hidden * hidden, axis=1, keepdims=True) + EPSILON)
    normed = (hidden * inv_rms * norm_gain[None, :]).astype(bf16)
    projected = jnp.dot(normed, full_weight, preferred_element_type=jnp.float32)
    step_raw = projected[:, 2 * local_inner + 2 * STATE :]
    gate = projected[:, :local_inner]
    conv_rows = projected[:, local_inner : 2 * local_inner + 2 * STATE].astype(bf16)
    sequence_starts = sequence_first_token.astype(jnp.float32)
    tail_rows, tail_flags = passed_along(
        (conv_rows[-width:], sequence_starts[-width:].astype(bf16)), 1
    )
    padded = jnp.concatenate([tail_rows, conv_rows], axis=0).astype(jnp.float32)
    flags_padded = jnp.concatenate([tail_flags.astype(jnp.float32), sequence_starts])
    conv_weight = jnp.concatenate([conv_inner_weight, conv_state_weight], axis=1)
    conv_bias = jnp.concatenate([conv_inner_bias, conv_state_bias])
    kept, final_state, final_product = mixer_front(
        padded,
        flags_padded,
        sequence_starts,
        step_raw,
        conv_weight,
        conv_bias,
        step_bias,
        decay_log,
    )
    carried = passed_along(final_state, 1)
    mixed = finish(kept, carried, skip_weight)
    gate_silu = jax.nn.silu(gate)
    gated = mixed * gate_silu
    grad_gated_normed = jnp.dot(output_cotangent, full_out_t, preferred_element_type=jnp.float32)
    scaled = grad_gated_normed * gate_gain[None, :]
    row_sums = lax.psum(
        jnp.stack([jnp.sum(gated * gated, axis=1), jnp.sum(gated * scaled, axis=1)]), "tp"
    )
    gate_inv = lax.rsqrt(row_sums[0] / INNER + EPSILON)[:, None]
    gated_normed = (gated * gate_inv * gate_gain[None, :]).astype(bf16)
    share = MODEL_WIDTH // lax.axis_size("tp")
    column = lax.axis_index("tp") * share
    branch = lax.psum_scatter(
        lax.dot_general(
            gated_normed, full_out_t, (((1,), (1,)), ((), ())), preferred_element_type=jnp.float32
        ).astype(bf16),
        "tp",
        scatter_dimension=1,
        tiled=True,
    )
    own_hidden = lax.dynamic_slice_in_dim(hidden, column, share, 1)
    block_output = (own_hidden + branch.astype(jnp.float32)).astype(bf16)
    grad_gated = gate_inv * scaled - gated * gate_inv**3 * (row_sums[1] / INNER)[:, None]
    grad_gain_gate = jnp.sum(grad_gated_normed * gated * gate_inv, axis=0)
    sigmoid_gate = jax.nn.sigmoid(gate)
    grad_mixed = grad_gated * gate_silu
    grad_gate = (
        grad_gated * mixed * sigmoid_gate * (1.0 + gate * (1.0 - sigmoid_gate))
    ).astype(bf16)
    grad_out = lax.dot_general(
        output_cotangent,
        gated_normed,
        (((0,), (0,)), ((), ())),
        preferred_element_type=jnp.float32,
    ).astype(bf16)
    grad_gate_weight = jnp.dot(
        normed.T, grad_gate, preferred_element_type=jnp.float32
    ).astype(bf16)
    first_grads = lax.psum_scatter(
        jnp.concatenate([grad_gate_weight, grad_out], axis=1),
        everyone,
        scatter_dimension=0,
        tiled=True,
    ).astype(jnp.float32)
    gate_grad = first_grads[:, :local_inner]
    out_proj_grad = first_grads[:, local_inner:].T

    def state_effect(carried_in):
        return finish(kept, carried_in, skip_weight)

    ignored, state_pull = jax.vjp(state_effect, carried)
    (through_mixed,) = state_pull(grad_mixed)
    next_grad = passed_along(through_mixed, -1)

    def full_mixer(padded_in, raw_in, weight_in, bias_in, step_in, decay_in, skip_in):
        return mixer(
            padded_in,
            flags_padded,
            sequence_starts,
            raw_in,
            weight_in,
            bias_in,
            step_in,
            decay_in,
            skip_in,
            carried,
        )

    ignored_out, pullback = jax.vjp(
        full_mixer,
        padded,
        step_raw,
        conv_weight,
        conv_bias,
        step_bias,
        decay_log,
        skip_weight,
    )
    (
        grad_padded,
        grad_step_raw,
        grad_conv_weight,
        grad_conv_bias,
        grad_step_bias,
        grad_decay_log,
        grad_skip,
    ) = pullback((grad_mixed, next_grad))
    returned = passed_along(grad_padded[:width], -1)
    grad_rows = grad_padded[width:]
    grad_rows = grad_rows.at[-width:].add(returned)
    grad_late = jnp.concatenate([grad_rows, grad_step_raw], axis=1).astype(bf16)
    grad_all = jnp.concatenate([grad_gate, grad_late], axis=1)
    tensor_part = lax.dot_general(
        grad_all, full_weight, (((1,), (1,)), ((), ())), preferred_element_type=jnp.float32
    )
    mean_sum = jnp.sum(hidden * norm_gain[None, :] * tensor_part, axis=1)
    own_grad = lax.psum_scatter(
        tensor_part.astype(bf16), "tp", scatter_dimension=1, tiled=True
    ).astype(jnp.float32)
    late_weight = jnp.dot(normed.T, grad_late, preferred_element_type=jnp.float32).astype(bf16)
    late_grads = lax.psum_scatter(
        late_weight, everyone, scatter_dimension=0, tiled=True
    ).astype(jnp.float32)
    mean_term = lax.psum(mean_sum, "tp")[:, None] / MODEL_WIDTH
    own_cotangent = lax.dynamic_slice_in_dim(output_cotangent, column, share, 1).astype(jnp.float32)
    own_gain = lax.dynamic_slice_in_dim(norm_gain, column, share, 0)
    input_grad = (
        own_cotangent
        + inv_rms * own_grad * own_gain[None, :]
        - own_hidden * inv_rms**3 * mean_term
    )
    grad_gain_norm = jnp.sum(own_grad * own_hidden * inv_rms, axis=0)
    parts = (
        grad_conv_weight[:, :local_inner],
        grad_conv_bias[:local_inner],
        grad_step_bias,
        grad_decay_log,
        grad_skip,
        grad_gain_gate,
        grad_gain_norm,
        grad_conv_weight[:, local_inner:],
        grad_conv_bias[local_inner:],
    )
    smalls = lax.psum(jnp.concatenate([p.reshape(-1) for p in parts]), everyone)
    split = []
    at = 0
    for p in parts:
        split.append(smalls[at : at + p.size])
        at += p.size
    state_flat = late_grads[:, local_inner : local_inner + 2 * STATE]
    shared = lax.psum(
        jnp.concatenate([split[7], split[8], state_flat.reshape(-1)]), "tp"
    )
    conv_state = shared[: KCONV * 2 * STATE].reshape(KCONV, 2 * STATE)
    bias_state = shared[KCONV * 2 * STATE : (KCONV + 1) * 2 * STATE]
    state_grad = shared[(KCONV + 1) * 2 * STATE :].reshape(state_flat.shape)
    return (
        block_output,
        input_grad,
        split[6],
        gate_grad,
        late_grads[:, :local_inner],
        late_grads[:, local_inner + 2 * STATE :],
        state_grad,
        split[0].reshape(KCONV, local_inner),
        split[1],
        conv_state,
        bias_state,
        split[2],
        split[3],
        split[4],
        split[5],
        out_proj_grad,
    )


def solution(mesh):
    return jax.shard_map(
        on_device,
        mesh=mesh,
        in_specs=(
            P(("dp", "ctx"), None),
            P(("dp", "ctx")),
            P(),
            P(("dp", "ctx"), "tp"),
            P(("dp", "ctx"), "tp"),
            P(("dp", "ctx"), "tp"),
            P(("dp", "ctx"), None),
            P(None, "tp"),
            P("tp"),
            P(),
            P(),
            P("tp"),
            P("tp"),
            P("tp"),
            P("tp"),
            P("tp", ("dp", "ctx")),
            P(("dp", "ctx"), None),
        ),
        out_specs=(
            P(("dp", "ctx"), "tp"),
            P(("dp", "ctx"), "tp"),
            P("tp"),
            P(("dp", "ctx"), "tp"),
            P(("dp", "ctx"), "tp"),
            P(("dp", "ctx"), "tp"),
            P(("dp", "ctx"), None),
            P(None, "tp"),
            P("tp"),
            P(),
            P(),
            P("tp"),
            P("tp"),
            P("tp"),
            P("tp"),
            P("tp", ("dp", "ctx")),
        ),
        check_vma=False,
    )
```

time: 840 us -> 459 us (0.55)
  waiting for transfers between devices: 343 us -> 186 us
  blocking collectives: 155 us -> 44.9 us
  matrix products: 116 us -> 67.2 us
  other arithmetic: 99.7 us -> 56 us
  local copies, waits for them, and re-layouts: 91.8 us -> 69.6 us
    reduce_scatter x6 -> x2, waiting for transfers between devices: 253 us -> 88 us  [the longest x1 45 us: on_device(): lax.psum_scatter(tensor_part.astype(bf16), 'tp', scatter_dimension=1, til...]
    psum x4 -> x3, blocking collectives: 128 us -> 44.9 us  [the longest x1 23.6 us: on_device(): smalls = lax.psum(jnp.concatenate([p.reshape(-1) for p in parts]), everyone)]
    dot_general x23 -> x21, matrix products: 116 us -> 67.2 us  [the longest x3 18.3 us: span_parts(): inner_mixed = jnp.einsum('ktsh,kshp->kthp', mixing, block_values)]
    unnamed x10 -> x9, waiting for transfers between devices: 1.73 us -> 45.4 us
    psum x1, waiting for transfers between devices: 74.6 us -> 31.3 us  [on_device(): lax.psum(jnp.concatenate([split[7], split[8], state_flat.reshape(-1)]), '...]
    all_gather x4 -> x0, blocking collectives: 24.3 us -> none  [the longest x1 10 us: on_device(): lax.all_gather(step_proj, ('dp', 'ctx'), axis=0, tiled=True)]
    dynamic_update_slice x20 -> x0, local copies, waits for them, and re-layouts: 18.2 us -> none  [fold_spans(): lax.scan(advance, init, (states, ends))]
    reshape x0 -> x8, local copies, waits for them, and re-layouts: none -> 13.6 us  [the longest x4 7.55 us: span_parts(): block_in = state_in.reshape(spans, SPAN, STATE)]
  transfers between devices with their start and end apart: 13 -> 12, of which waited for: 9 -> 6; matrix products, arithmetic and copies ran while one was open for 18% -> 21% of each run, Pallas kernels for 0% -> 0%
where the time goes in v1:
time: 459 us; the launch traced here: 451 us
  waiting for transfers between devices  186 us (41%)
  local copies, waits for them, and re-layouts  69.6 us (15%)
  matrix products  67.2 us (15%)
  other arithmetic  56 us (12%)
  blocking collectives  44.9 us (10%)
  between operations  16.2 us (4%)
  starting transfers between devices  10.6 us (2%)
    unnamed x9, waiting for transfers between devices  45.4 us
    reduce_scatter x1, waiting for transfers between devices, on_device(): lax.psum_scatter(tensor_part.astype(bf16), 'tp', scatter_dimension=1, til...  45 us
    reduce_scatter x1, waiting for transfers between devices, on_device(): lax.psum_scatter(lax.dot_general(gated_normed, full_out_t, (((1,), (1,)),...  43 us
    psum x1, waiting for transfers between devices, on_device(): lax.psum(jnp.concatenate([split[7], split[8], state_flat.reshape(-1)]), '...  31.3 us
    psum x1, blocking collectives, on_device(): smalls = lax.psum(jnp.concatenate([p.reshape(-1) for p in parts]), everyone)  23.6 us
    unnamed x254, local copies, waits for them, and re-layouts  22.9 us
    all_gather x1, waiting for transfers between devices, on_device(): lax.all_gather(jnp.concatenate([gate_proj, input_proj, state_proj, step_p...  21.5 us
    dot_general x3, matrix products, span_parts(): inner_mixed = jnp.einsum('ktsh,kshp->kthp', mixing, block_values)  18.3 us
  transfers between devices with their start and end apart: 12, of which 6 were waited for; matrix products, arithmetic and copies ran while one was open for 21% of the time, Pallas kernels for 0%

profile of v1, /device:TPU:0, one launch (start us, length us, event | category | flops | bytes accessed | tf_op | source)
XLA Modules:
  0.0 450.7 jit_solution(5405197724828747392)
XLA Ops:
  8.3 1.8 pad_maximum_fusion.1
  10.9 2.4 collective-permute-start.1
  13.4 2.1 multiply_reduce_fusion.2
  22.9 21.5 %all-gather.3.cloned.1.call-done = bf16[1024,1288]{1,0:T(8,128)(2,1)} async-done(((bf16[128,1288]{1,0:T(8,128)(2,1)}), bf16[1024,1288]{1,0:T(8,128)(2,1)}) %all-gather.3.cloned.1.call-update) | async-done | bytes 2637840 | tf_op jit(solution)/shard_map/all_gather | solution.py:161
  44.4 5.0 %fusion.158 = (bf16[1024,1288]{0,1:T(8,128)(2,1)S(1)}, f32[1024,1288]{0,1:T(8,128)S(1)}) fusion(bf16[1024,1288]{1,0:T(8,128)(2,1)} %all-gather.3.cloned.1.call-done, bf16[1024,1024]{1,0:T(8,128)(2,1)S(1)} %copy-done.12, f32[1024]{0:T(1024)S(1)} %copy-done.112, f32[1024]{0:T(1024)S(1)} %get-tuple-element.170), kind=kOutput, calls=%fused_computation.265 | convolution fusion | flops 2706644992 | bytes 12656640 | tf_op jit(solution)/shard_map/dot_general | solution.py:171
  49.6 2.2 collective-permute-start
  55.4 4.7 %fusion.24 = (f32[1024,768]{0,1:T(8,128)S(1)}, f32[1024,768]{0,1:T(8,128)}) fusion(f32[1024]{0:T(1024)S(1)} %get-tuple-element.166, f32[1027,768]{0,1:T(8,128)S(1)} %maximum_convert_fusion, f32[768]{0:T(1024)S(1)} %copy-done.53, f32[1024]{0:T(1024)S(1)} %get-tuple-element.167, f32[768]{0:T(1024)S(1)} %copy-done.55, f32[1024]{0:T(1024)S(1)} %copy-done.47, ...), kind=kLoop, calls=%fused_computation.37 | loop fusion | flops 12582912 | bytes 18906112 | tf_op jit(solution)/shard_map/jit(silu)/mul | solution.py:85
  60.1 1.7 slice.363
  63.2 3.2 reshape.485
  66.5 1.8 reshape.490
  68.3 1.8 copy.168
  70.1 3.1 fusion.42
  73.2 1.8 copy.138
  75.0 2.1 fusion.92
  77.2 2.3 collective-permute-start.2
  79.5 1.8 reshape.489
  81.3 1.8 copy.137
  83.1 1.8 copy.169
  84.9 1.3 multiply_add_fusion.2
  86.3 1.6 fusion.159
  88.0 1.6 fusion.81
  89.7 3.3 fusion.34
  93.1 1.4 copy.145
  94.4 1.8 copy.193
  96.3 6.8 %multiply_reduce_fusion.12 = (f32[1024]{0:T(1024)S(1)}, f32[1024]{0:T(1024)S(1)}, f32[1024,512]{0,1:T(8,128)}, f32[1024,512]{0,1:T(8,128)}) fusion(f32[512]{0:T(512)} %param.33, f32[1024,512]{0,1:T(8,128)} %bitcast.219, f32[1024,1288]{0,1:T(8,128)} %copy-done.33, bf16[1024,1024]{1,0:T(8,128)(2,1)} %param.35, bf16[1024,512]{0,1:T(8,128)(2,1)} %all-gather.5.cloned.1.call-done), kind=kOutput, calls=%fused_computation.65 | convolution fusion | flops 1078982656 | bytes 11544576 | tf_op jit(solution)/shard_map/dot_general | solution.py:197
  103.7 12.9 %psum.28 = f32[2,1024]{1,0:T(2,128)} all-reduce(f32[2,1024]{1,0:T(2,128)} %pad_maximum_fusion.3), channel_id=1, replica_groups=mesh['dp'=4,'ctx'=2,'tp'=4] {'tp'}, use_global_device_ids=true, to_apply=%region_7.8 | all-reduce | flops 2048 | bytes 16384 | tf_op jit(solution)/shard_map/psum | solution.py:199
  117.4 6.6 %multiply_reduce_fusion.8 = (f32[512]{0:T(512)}, f32[1024,512]{0,1:T(8,128)}, bf16[1024,512]{0,1:T(8,128)(2,1)}, f32[512]{0:T(512)}) fusion(f32[1024,768]{0,1:T(8,128)} %copy-done.8, f32[1024,1288]{0,1:T(8,128)} %copy-done.33, f32[1024]{0:T(1024)S(1)} %bitcast.251, f32[1024,512]{0,1:T(8,128)} %get-tuple-element.128, f32[1024]{0:T(1024)S(1)} %multiply_multiply_fusion.5, ...), kind=kLoop, calls=%fused_computation.57 | loop fusion | flops 11533312 | bytes 13649920 | tf_op jit(solution)/shard_map/transpose(jvp())/reduce_sum | solution.py:107
  124.1 3.2 reshape.492
  127.3 9.8 %fusion.9 = (f32[4,256,8]{1,2,0:T(8,128)}, f32[4,256,8]{1,2,0:T(8,128)}, f32[4,256,8]{1,2,0:T(8,128)}, bf16[4,256,256]{2,1,0:T(8,128)(2,1)S(1)}) fusion(f32[4,256,8]{1,2,0:T(8,128)} %bitcast.234, f32[4,256,256]{2,1,0:T(8,128)} %copy-done.31, f32[4,256,8]{1,2,0:T(8,128)} %copy-done.42, pred[4,256,256]{2,1,0:T(8,128)(4,1)} %compare_and_fusion, ...), kind=kOutput, calls=%fused_computation.13 | convolution fusion | flops 299606016 | bytes 6193152 | tf_op jit(solution)/shard_map/transpose(jvp(ktsh,kshp->kthp))/dot_general | solution.py:58
  137.5 2.6 fusion.68
  140.0 2.0 copy.181
  142.1 3.1 multiply_reduce_fusion.13
  145.2 1.7 collective-permute-start.3
  146.9 2.8 multiply_reduce_fusion.9
  149.7 1.9 multiply_reduce_fusion.18
  152.6 2.6 multiply_reduce_fusion.10
  156.3 2.0 copy.184
  158.4 5.2 %bitcast_add_fusion = f32[4,256,8,64]{1,3,2,0:T(8,128)S(1)} fusion(f32[4,256,8,64]{1,3,2,0:T(8,128)} %get-tuple-element.183, f32[4,256,8]{1,2,0:T(8,128)} %bitcast.235, f32[4,256,256]{2,1,0:T(8,128)} %copy-done.31, f32[4,256,8]{1,2,0:T(8,128)} %copy-done.42, pred[4,256,256]{2,1,0:T(8,128)(4,1)} %compare_and_fusion, f32[4,256,8,64]{1,0,3,2:T(4,128)} %reshape.492, ...), kind=kOutput, calls=%fused_computation.50 | convolution fusion | flops 279969792 | bytes 7700480 | tf_op jit(solution)/shard_map/transpose(jvp(ktsh,kshp->kthp))/dot_general | solution.py:58
  163.5 1.4 copy.157
  166.8 1.6 copy-done.10
  168.7 5.3 %multiply_reduce_fusion.6 = (f32[768]{0:T(1024)}, f32[768]{0:T(1024)}, f32[768]{0:T(1024)}, f32[768]{0:T(1024)}, f32[768]{0:T(1024)}, /*index=5*/f32[1024,768]{0,1:T(8,128)S(1)}) fusion(f32[1027,768]{0,1:T(8,128)S(1)} %maximum_convert_fusion, f32[1024]{0:T(1024)S(1)} %get-tuple-element.166, f32[1024]{0:T(1024)S(1)} %get-tuple-element.167, ...), kind=kLoop, calls=%fused_computation.35 | loop fusion | flops 18870528 | bytes 22051840 | tf_op jit(solution)/shard_map/transpose(jvp())/reduce_sum | solution.py:34
  175.2 1.3 pad_add_fusion.4
  179.2 4.1 pad_add_fusion
  183.3 1.5 collective-permute-start.4
  186.9 3.3 slice.381
  190.2 1.6 add_add_fusion
  191.8 3.1 scatter-add.4
  195.0 5.3 %convolution_convert_fusion.1 = bf16[1024,776]{0,1:T(8,128)(2,1)} fusion(bf16[1024,8]{0,1:T(8,128)(2,1)S(1)} %get-tuple-element.122, bf16[1024,768]{0,1:T(8,128)(2,1)} %scatter-add.4, bf16[1024,1024]{1,0:T(8,128)(2,1)} %param.19, f32[1024]{0:T(1024)S(1)} %copy-done.113, f32[1024]{0:T(1024)S(1)} %copy-done.71), kind=kOutput, calls=%fused_computation.78 | convolution fusion | flops 1635557376 | bytes 5283840 | tf_op jit(solution)/shard_map/dot_general | solution.py:293
  200.3 3.9 copy.189
  204.3 1.4 convolution_convert_fusion.2
  206.4 1.3 fusion.61
  207.7 1.5 pad_maximum_fusion
  209.3 4.0 copy.187
  213.4 4.7 %convolution_convert_fusion = bf16[1024,1024]{1,0:T(8,128)(2,1)} fusion(bf16[1024,512]{0,1:T(8,128)(2,1)} %all-gather.5.cloned.1.call-done, f32[1024,512]{0,1:T(8,128)} %get-tuple-element.128, f32[1024]{0:T(1024)S(1)} %bitcast.246, f32[512]{0:T(512)S(1)} %copy-done.98), kind=kOutput, calls=%fused_computation.76 | convolution fusion | flops 1076363264 | bytes 5249024 | tf_op jit(solution)/shard_map/dot_general | solution.py:207
  218.2 7.2 %multiply_reduce_fusion.1 = (f32[1024]{0:T(1024)S(1)}, bf16[1024,1024]{1,0:T(8,128)(2,1)}) fusion(bf16[1024,1024]{1,0:T(8,128)(2,1)S(1)} %copy-done.13, f32[1024]{0:T(1024)S(1)} %copy-done.113, bf16[1024,1288]{1,0:T(8,128)(2,1)} %all-gather.3.cloned.1.call-done, bf16[1024,8]{0,1:T(8,128)(2,1)S(1)} %get-tuple-element.122, bf16[1024,768]{0,1:T(8,128)(2,1)} %scatter-add.4, ...), kind=kOutput, calls=%fused_computation.14 | convolution fusion | flops 2714287104 | bytes 9478144 | tf_op jit(solution)/shard_map/dot_general | solution.py:286
  225.8 2.4 convert_element_type.76
  228.7 8.4 %psum.29 = f32[1024]{0:T(1024)S(1)} all-reduce(f32[1024]{0:T(1024)S(1)} %get-tuple-element.145), channel_id=1, replica_groups=mesh['dp'=4,'ctx'=2,'tp'=4] {'tp'}, use_global_device_ids=true, to_apply=%region_25.26 | all-reduce | flops 1024 | bytes 8192 | tf_op jit(solution)/shard_map/psum | solution.py:297
  237.1 5.4 %reduce-scatter.15.cloned.1.call-done = bf16[128,776]{1,0:T(8,128)(2,1)} async-done(((bf16[1024,776]{1,0:T(8,128)(2,1)}), bf16[128,776]{1,0:T(8,128)(2,1)}) %reduce-scatter.15.cloned.1.call-update) | async-done | bytes 198672
  247.0 39.8 %reduce-scatter.13.cloned.1.call-done = bf16[128,1024]{1,0:T(8,128)(2,1)} async-done(((bf16[1024,1024]{1,0:T(8,128)(2,1)}), bf16[128,1024]{1,0:T(8,128)(2,1)}) %reduce-scatter.13.cloned.1.call-update) | async-done | bytes 262160
  289.6 43.0 %reduce-scatter.9.cloned.1.call-done = bf16[1024,256]{1,0:T(8,128)(2,1)} async-done(((bf16[1024,1024]{1,0:T(8,128)(2,1)}), bf16[1024,256]{1,0:T(8,128)(2,1)}) %reduce-scatter.9.cloned.1.call-update) | async-done | bytes 524304 | tf_op jit(solution)/shard_map/reduce_scatter | solution.py:206
  332.7 45.0 %reduce-scatter.11.cloned.1.call-done = bf16[1024,256]{1,0:T(8,128)(2,1)} async-done(((bf16[1024,1024]{1,0:T(8,128)(2,1)}), bf16[1024,256]{1,0:T(8,128)(2,1)}) %reduce-scatter.11.cloned.1.call-update) | async-done | bytes 524304 | tf_op jit(solution)/shard_map/reduce_scatter | solution.py:290
  377.7 3.4 fusion.75
  381.2 23.6 %psum.30 = f32[4632]{0:T(1024)S(1)} all-reduce(f32[4632]{0:T(1024)S(1)} %concatenate.41), channel_id=1, replica_groups=mesh['dp'=4,'ctx'=2,'tp'=4] {'dp','ctx'}, use_global_device_ids=true, to_apply=%region_37.38 | all-reduce | flops 4632 | bytes 37056 | tf_op jit(solution)/shard_map/psum | solution.py:317
  408.0 31.3 %all-reduce.28.cloned.1.call-done = f32[34048]{0:T(1024)} async-done(((f32[34048]{0:T(1024)}), f32[34048]{0:T(1024)}) %all-reduce.28.cloned.1.call-update) | async-done | bytes 136208 | tf_op jit(solution)/shard_map/psum | solution.py:324
  (364 shorter events, 42.4 us)
Async XLA Ops:
  7.2 37.2 %copy-start.12 = (bf16[1024,1024]{1,0:T(8,128)(2,1)S(1)}, bf16[1024,1024]{1,0:T(8,128)(2,1)}, u32[]{:S(2)}) copy-start(bf16[1024,1024]{1,0:T(8,128)(2,1)} %param.19) | copy-start | bytes 6291460
  7.2 8.9 %copy-start.84 = (f32[4,512]{1,0:T(4,128)S(1)}, f32[4,512]{1,0:T(4,128)}, u32[]{:S(2)}) copy-start(f32[4,512]{1,0:T(4,128)} %param.26) | copy-start | bytes 24580
  7.2 8.9 %copy-start.97 = (f32[4,256]{1,0:T(4,128)S(1)}, f32[4,256]{1,0:T(4,128)}, u32[]{:S(2)}) copy-start(f32[4,256]{1,0:T(4,128)} %param.28) | copy-start | bytes 12292
  7.2 9.5 %copy-start.114 = (f32[8]{0:T(128)S(1)}, f32[8]{0:T(128)}, u32[]{:S(2)}) copy-start(f32[8]{0:T(128)} %param.31) | copy-start | bytes 100
  7.2 12.9 %copy-start.110 = (f32[8]{0:T(128)S(1)}, f32[8]{0:T(128)}, u32[]{:S(2)}) copy-start(f32[8]{0:T(128)} %param.32) | copy-start | bytes 100
  7.2 13.7 %copy-start.103 = (f32[512]{0:T(512)S(1)}, f32[512]{0:T(512)}, u32[]{:S(2)}) copy-start(f32[512]{0:T(512)} %param.27) | copy-start | bytes 6148
  7.2 13.7 %copy-start.109 = (f32[256]{0:T(256)S(1)}, f32[256]{0:T(256)}, u32[]{:S(2)}) copy-start(f32[256]{0:T(256)} %param.29) | copy-start | bytes 3076
  7.3 37.2 %copy-start.112 = (f32[1024]{0:T(1024)S(1)}, f32[1024]{0:T(1024)}, u32[]{:S(2)}) copy-start(f32[1024]{0:T(1024)} %param.21) | copy-start | bytes 12292
  7.3 37.2 %all-gather.3.cloned.1.call-start = ((), (), s32[]{:S(2)}) async-start(), calls=%async_computation.4 | async-start | bytes 3244032 | tf_op jit(solution)/shard_map/all_gather | solution.py:161
  10.1 86.2 %all-gather.5.cloned.1.call-start = ((), (), s32[]{:S(2)}) async-start(), calls=%async_computation.5 | async-start | bytes 1179648 | tf_op jit(solution)/shard_map/all_gather | solution.py:167
  10.9 10.6 %collective-permute-start.1 = (bf16[3]{0:T(256)(128)(2,1)S(1)}, bf16[3]{0:T(256)(128)(2,1)S(1)}, u32[]{:S(2)}, u32[]{:S(2)}) collective-permute-start(bf16[3]{0:T(256)(128)(2,1)S(1)} %slice.286), channel_id=1, source_target_pairs={{0,4},{1,5},{2,6},{3,7},{8,12},{9,13},{10,14},{11,15},{16,20},{17,... | collective-permute-start | bytes 26 | tf_op jit(solution)/shard_map/ppermute | solution.py:21
  13.3 229.2 %reduce-scatter.15.cloned.1.call-start = ((), (), s32[]{:S(2)}) async-start(), calls=%async_computation.10 | async-start | bytes 2064384
  16.1 33.4 %copy-start.70 = (f32[1024]{0:T(1024)}, f32[1024]{0:T(1024)S(1)}, u32[]{:S(2)}) copy-start(f32[1024]{0:T(1024)S(1)} %get-tuple-element.170) | copy-start | bytes 12292
  16.7 35.0 %copy-start.101 = (f32[8]{0:T(128)}, f32[8]{0:T(128)S(1)}, u32[]{:S(2)}) copy-start(f32[8]{0:T(128)S(1)} %exponential_negate_fusion) | copy-start | bytes 100
  18.6 33.8 %copy-start.78 = (pred[4,256]{1,0:T(4,128)(4,1)}, pred[4,256]{1,0:T(4,128)(4,1)S(1)}, u32[]{:S(2)}) copy-start(pred[4,256]{1,0:T(4,128)(4,1)S(1)} %get-tuple-element.172) | copy-start | bytes 3076
  18.6 33.8 %copy-start.95 = (pred[4,256]{1,0:T(4,128)(4,1)}, pred[4,256]{1,0:T(4,128)(4,1)S(1)}, u32[]{:S(2)}) copy-start(pred[4,256]{1,0:T(4,128)(4,1)S(1)} %get-tuple-element.171) | copy-start | bytes 3076
  44.4 7.3 %copy-start.99 = (f32[8]{0:T(128)S(1)}, f32[8]{0:T(128)}, u32[]{:S(2)}) copy-start(f32[8]{0:T(128)} %param.30) | copy-start | bytes 100
  49.5 5.9 %copy-start.33 = (f32[1024,1288]{0,1:T(8,128)}, f32[1024,1288]{0,1:T(8,128)S(1)}, u32[]{:S(2)}) copy-start(f32[1024,1288]{0,1:T(8,128)S(1)} %get-tuple-element.179) | copy-start | bytes 15826948
  49.6 4.9 %collective-permute-start = (bf16[3,768]{0,1:T(8,128)(2,1)S(1)}, bf16[3,768]{0,1:T(8,128)(2,1)S(1)}, u32[]{:S(2)}, u32[]{:S(2)}) collective-permute-start(bf16[3,768]{0,1:T(8,128)(2,1)S(1)} %slice.348), channel_id=1, source_target_pairs={{0,4},{1,5},{2,6},{3,7},{8,12},{9,13},{10,14},{11,15},{16,20},{17,... | collective-permute-start | bytes 13832 | tf_op jit(solution)/shard_map/ppermute | solution.py:21
  77.2 10.8 %collective-permute-start.2 = (f32[8,64,128]{2,1,0:T(8,128)}, f32[8,64,128]{2,1,0:T(8,128)}, u32[]{:S(2)}, u32[]{:S(2)}) collective-permute-start(f32[8,64,128]{2,1,0:T(8,128)} %get-tuple-element.131), channel_id=1, source_target_pairs={{0,4},{1,5},{2,6},{3,7},{8,12},{9,13},{10,14},{11,15},{16,20},{17,... | collective-permute-start | bytes 786440 | tf_op jit(solution)/shard_map/ppermute | solution.py:21
  117.4 6.7 %copy-start.49 = (f32[1,1024]{1,0:T(1,128)}, f32[1,1024]{1,0:T(1,128)S(1)}, u32[]{:S(2)}) copy-start(f32[1,1024]{1,0:T(1,128)S(1)} %get-tuple-element.164) | copy-start | bytes 12292
  127.2 9.9 %copy-start.23 = (bf16[4,256,128]{2,1,0:T(8,128)(2,1)S(1)}, bf16[4,256,128]{2,1,0:T(8,128)(2,1)}, u32[]{:S(2)}) copy-start(bf16[4,256,128]{2,1,0:T(8,128)(2,1)} %copy.138) | copy-start | bytes 786436
  127.2 10.2 %copy-start.6 = (f32[4,256,8,64]{1,0,3,2:T(4,128)S(1)}, f32[4,256,8,64]{1,0,3,2:T(4,128)}, u32[]{:S(2)}) copy-start(f32[4,256,8,64]{1,0,3,2:T(4,128)} %reshape.492) | copy-start | bytes 6291460
  127.3 10.2 %copy-start.16 = (f32[1,8,64,128]{3,2,1,0:T(8,128)S(1)}, f32[1,8,64,128]{3,2,1,0:T(8,128)}, u32[]{:S(2)}) copy-start(f32[1,8,64,128]{3,2,1,0:T(8,128)} %copy-done.15) | copy-start | bytes 786436
  127.3 10.2 %copy-start.18 = (f32[1,8,64,128]{3,2,1,0:T(8,128)S(1)}, f32[1,8,64,128]{3,2,1,0:T(8,128)}, u32[]{:S(2)}) copy-start(f32[1,8,64,128]{3,2,1,0:T(8,128)} %copy-done.17) | copy-start | bytes 786436
  127.3 10.2 %copy-start.20 = (f32[1,8,64,128]{3,2,1,0:T(8,128)S(1)}, f32[1,8,64,128]{3,2,1,0:T(8,128)}, u32[]{:S(2)}) copy-start(f32[1,8,64,128]{3,2,1,0:T(8,128)} %copy-done.19) | copy-start | bytes 786436
  127.3 10.2 %copy-start.39 = (f32[4,256,8]{1,2,0:T(8,128)S(1)}, f32[4,256,8]{1,2,0:T(8,128)}, u32[]{:S(2)}) copy-start(f32[4,256,8]{1,2,0:T(8,128)} %copy-done.37) | copy-start | bytes 98308
  127.3 10.2 %copy-start.77 = (f32[4]{0:T(128)S(1)}, f32[4]{0:T(128)}, u32[]{:S(2)}) copy-start(f32[4]{0:T(128)} %pad.121.clone) | copy-start | bytes 52
  145.2 6.6 %copy-start.5 = (f32[4,256,8,64]{1,0,3,2:T(4,128)S(1)}, f32[4,256,8,64]{1,0,3,2:T(4,128)}, u32[]{:S(2)}) copy-start(f32[4,256,8,64]{1,0,3,2:T(4,128)} %reshape.485) | copy-start | bytes 6291460
  145.2 6.6 %copy-start.40 = (f32[4,256,8]{1,2,0:T(8,128)S(1)}, f32[4,256,8]{1,2,0:T(8,128)}, u32[]{:S(2)}) copy-start(f32[4,256,8]{1,2,0:T(8,128)} %get-tuple-element.157) | copy-start | bytes 98308
  145.2 4.5 %collective-permute-start.3 = (f32[8,64,128]{2,1,0:T(8,128)S(1)}, f32[8,64,128]{2,1,0:T(8,128)S(1)}, u32[]{:S(2)}, u32[]{:S(2)}) collective-permute-start(f32[8,64,128]{2,1,0:T(8,128)S(1)} %get-tuple-element.106), channel_id=1, source_target_pairs={{4,0},{5,1},{6,2},{7,3},{12,8},{13,9},{14,10},{15,11},{20,16},{21,... | collective-permute-start | bytes 786440 | tf_op jit(solution)/shard_map/ppermute | solution.py:21
  168.7 5.3 %copy-start.56 = (f32[768]{0:T(1024)S(1)}, f32[768]{0:T(1024)}, u32[]{:S(2)}) copy-start(f32[768]{0:T(1024)} %get-tuple-element.117) | copy-start | bytes 9220
  179.0 5.9 %copy-start.89 = (f32[8]{0:T(128)S(1)}, f32[8]{0:T(128)}, u32[]{:S(2)}) copy-start(f32[8]{0:T(128)} %get-tuple-element.111) | copy-start | bytes 100
  179.0 5.9 %copy-start.90 = (f32[4,8]{1,0:T(4,128)S(1)}, f32[4,8]{1,0:T(4,128)}, u32[]{:S(2)}) copy-start(f32[4,8]{1,0:T(4,128)} %get-tuple-element.105) | copy-start | bytes 388
  179.0 5.9 %copy-start.92 = (f32[1,8]{1,0:T(1,128)S(1)}, f32[1,8]{1,0:T(1,128)}, u32[]{:S(2)}) copy-start(f32[1,8]{1,0:T(1,128)} %copy-done.91) | copy-start | bytes 100
  179.0 5.9 %copy-start.94 = (f32[1,8]{1,0:T(1,128)S(1)}, f32[1,8]{1,0:T(1,128)}, u32[]{:S(2)}) copy-start(f32[1,8]{1,0:T(1,128)} %copy-done.93) | copy-start | bytes 100
  179.0 5.9 %copy-start.108 = (f32[8]{0:T(128)S(1)}, f32[8]{0:T(128)}, u32[]{:S(2)}) copy-start(f32[8]{0:T(128)} %get-tuple-element.109) | copy-start | bytes 100
  179.0 5.9 %copy-start.68 = (f32[8]{0:T(128)S(1)}, f32[8]{0:T(128)}, u32[]{:S(2)}) copy-start(f32[8]{0:T(128)} %copy-done.66) | copy-start | bytes 100
  179.0 5.9 %copy-start.86 = (f32[8]{0:T(128)S(1)}, f32[8]{0:T(128)}, u32[]{:S(2)}) copy-start(f32[8]{0:T(128)} %copy-done.85) | copy-start | bytes 100
  179.0 5.9 %copy-start.104 = (f32[8]{0:T(128)S(1)}, f32[8]{0:T(128)}, u32[]{:S(2)}) copy-start(f32[8]{0:T(128)} %get-tuple-element.103) | copy-start | bytes 100
  179.0 5.9 %copy-start.105 = (f32[8]{0:T(128)S(1)}, f32[8]{0:T(128)}, u32[]{:S(2)}) copy-start(f32[8]{0:T(128)} %get-tuple-element.104) | copy-start | bytes 100
  179.1 5.9 %copy-start.106 = (f32[8]{0:T(128)S(1)}, f32[8]{0:T(128)}, u32[]{:S(2)}) copy-start(f32[8]{0:T(128)} %get-tuple-element.107) | copy-start | bytes 100
  179.1 5.9 %copy-start.107 = (f32[8]{0:T(128)S(1)}, f32[8]{0:T(128)}, u32[]{:S(2)}) copy-start(f32[8]{0:T(128)} %get-tuple-element.108) | copy-start | bytes 100
  179.1 6.0 %copy-start.36 = (f32[1024,8]{0,1:T(8,128)S(1)}, f32[1024,8]{0,1:T(8,128)}, u32[]{:S(2)}) copy-start(f32[1024,8]{0,1:T(8,128)} %copy-done.34) | copy-start | bytes 98308
  179.1 6.0 %copy-start.44 = (f32[4,256,8]{1,2,0:T(8,128)S(1)}, f32[4,256,8]{1,2,0:T(8,128)}, u32[]{:S(2)}) copy-start(f32[4,256,8]{1,2,0:T(8,128)} %copy-done.42) | copy-start | bytes 98308
  179.1 6.0 %copy-start.45 = (f32[4,256,8]{1,2,0:T(8,128)S(1)}, f32[4,256,8]{1,2,0:T(8,128)}, u32[]{:S(2)}) copy-start(f32[4,256,8]{1,2,0:T(8,128)} %get-tuple-element.182) | copy-start | bytes 98308
  179.1 6.0 %copy-start.60 = (f32[4,256,8]{1,2,0:T(8,128)S(1)}, f32[4,256,8]{1,2,0:T(8,128)}, u32[]{:S(2)}) copy-start(f32[4,256,8]{1,2,0:T(8,128)} %get-tuple-element.94) | copy-start | bytes 98308
  179.1 6.0 %copy-start.65 = (f32[4,8]{1,0:T(4,128)S(1)}, f32[4,8]{1,0:T(4,128)}, u32[]{:S(2)}) copy-start(f32[4,8]{1,0:T(4,128)} %copy-done.64) | copy-start | bytes 388
  179.1 6.0 %copy-start.79 = (pred[4,256]{1,0:T(4,128)(4,1)S(1)}, pred[4,256]{1,0:T(4,128)(4,1)}, u32[]{:S(2)}) copy-start(pred[4,256]{1,0:T(4,128)(4,1)} %copy-done.78) | copy-start | bytes 3076
  179.1 6.3 %copy-start.59 = (f32[4,256,8]{1,2,0:T(8,128)S(1)}, f32[4,256,8]{1,2,0:T(8,128)}, u32[]{:S(2)}) copy-start(f32[4,256,8]{1,2,0:T(8,128)} %multiply_reduce_fusion.9) | copy-start | bytes 98308
  179.2 6.3 %copy-start.96 = (pred[4,256]{1,0:T(4,128)(4,1)S(1)}, pred[4,256]{1,0:T(4,128)(4,1)}, u32[]{:S(2)}) copy-start(pred[4,256]{1,0:T(4,128)(4,1)} %copy-done.95) | copy-start | bytes 3076
  179.2 6.3 %copy-start.116 = (f32[4,256,8]{1,2,0:T(8,128)S(1)}, f32[4,256,8]{1,2,0:T(8,128)}, u32[]{:S(2)}) copy-start(f32[4,256,8]{1,2,0:T(8,128)} %get-tuple-element.92) | copy-start | bytes 98308
  179.2 6.3 %copy-start.117 = (f32[4,256,8]{1,2,0:T(8,128)S(1)}, f32[4,256,8]{1,2,0:T(8,128)}, u32[]{:S(2)}) copy-start(f32[4,256,8]{1,2,0:T(8,128)} %get-tuple-element.93) | copy-start | bytes 98308
  179.2 6.5 %copy-start.100 = (f32[8]{0:T(128)S(1)}, f32[8]{0:T(128)}, u32[]{:S(2)}) copy-start(f32[8]{0:T(128)} %param.30) | copy-start | bytes 100
  179.2 6.5 %copy-start.102 = (f32[8]{0:T(128)S(1)}, f32[8]{0:T(128)}, u32[]{:S(2)}) copy-start(f32[8]{0:T(128)} %copy-done.101) | copy-start | bytes 100
  183.3 6.9 %collective-permute-start.4 = (f32[3,768]{0,1:T(8,128)}, f32[3,768]{0,1:T(8,128)}, u32[]{:S(2)}, u32[]{:S(2)}) collective-permute-start(f32[3,768]{0,1:T(8,128)} %pad_add_fusion.4), channel_id=1, source_target_pairs={{4,0},{5,1},{6,2},{7,3},{12,8},{13,9},{14,10},{15,11},{20,16},{21,... | collective-permute-start | bytes 27656 | tf_op jit(solution)/shard_map/ppermute | solution.py:21
  204.1 82.7 %reduce-scatter.13.cloned.1.call-start = ((), (), s32[]{:S(2)}) async-start(), calls=%async_computation.9 | async-start | bytes 2359296
  213.3 119.3 %reduce-scatter.9.cloned.1.call-start = ((), (), s32[]{:S(2)}) async-start(), calls=%async_computation.6 | async-start | bytes 2621440 | tf_op jit(solution)/shard_map/reduce_scatter | solution.py:206
  218.1 159.5 %reduce-scatter.11.cloned.1.call-start = ((), (), s32[]{:S(2)}) async-start(), calls=%async_computation.7 | async-start | bytes 2621440 | tf_op jit(solution)/shard_map/reduce_scatter | solution.py:290
  225.4 213.9 %all-reduce.28.cloned.1.call-start = ((), (), s32[]{:S(2)}) async-start(), calls=%async_computation.8 | async-start | bytes 278528 | tf_op jit(solution)/shard_map/psum | solution.py:324
  228.5 61.1 %copy-start.80 = (f32[1,768]{1,0:T(1,128)}, f32[1,768]{1,0:T(1,128)S(1)}, u32[]{:S(2)}) copy-start(f32[1,768]{1,0:T(1,128)S(1)} %reshape.503) | copy-start | bytes 9220
  228.7 149.0 %copy-start.69 = (f32[1024]{0:T(1024)S(1)}, f32[1024]{0:T(1024)}, u32[]{:S(2)}) copy-start(f32[1024]{0:T(1024)} %get-tuple-element.169) | copy-start | bytes 12292
  288.0 93.1 %copy-start.81 = (f32[512]{0:T(512)S(1)}, f32[512]{0:T(512)}, u32[]{:S(2)}) copy-start(f32[512]{0:T(512)} %get-tuple-element.143) | copy-start | bytes 6148
  332.6 48.4 %slice-start = ((f32[1,768]{1,0:T(1,128)}), f32[1,512]{1,0:T(1,128)S(1)}, s32[]{:S(2)}) async-start(f32[1,768]{1,0:T(1,128)} %copy-done.80), calls=%async_computation.11 | async-start | bytes 4096 | tf_op jit(solution)/shard_map/slice | solution.py:308
  (67 other events, 180.1 us)
Sparse Core Ops, SparseCore 0:
  10.5 33.8 all-gather.2
  46.3 23.5 all-gather.4
  204.3 38.2 reduce-scatter.14
  245.7 41.1 reduce-scatter.12
  289.0 43.6 reduce-scatter.8
  334.8 42.8 reduce-scatter.10
  406.9 32.2 all-reduce.27
